TPU v7x, 32 devices: a whole 2x2x4 slice. The times are simulated.
32 devices in a mesh: lon: 8 (over z, x), lat: 4 (over y, core).
Axes of the slice: x: 2, y: 2, z: 4, core: 2. Of those that a mesh axis runs over, the one named last changes fastest.
Arguments:
- control_fields: float32 [2, 4, 544, 1536], P(None, None, 'lon', 'lat'), may hold values from -4 to 4
- unexplained_elevation: float32 [544, 1536], P('lon', 'lat'), may hold values from -6 to 6
- diffusivity: float32 [544, 1536], P('lon', 'lat'), may hold values from 0.15 to 0.49
- depth_levels: int32 [544, 1536], P('lon', 'lat'), may hold values from 0 to 4
- fold_partner: int32 [544], replicated, may hold values from 0 to 543, as said below
- prior_sigmas: float32 [2, 4], replicated, may hold values from 0.5 to 2
- haline_thermal_ratio: float32 [544, 1536], P('lon', 'lat'), may hold values from -0.6 to 0.6
- expansion_coefficients: float32 [2, 4], replicated, may hold values from -3 to 3
Outputs:
- state_fields: float32 [2, 4, 544, 1536], P(None, None, 'lon', 'lat')
- sea_height: float32 [544, 1536], P('lon', 'lat')
Inputs may be any that keep to these rules, and one draw needn't show every extreme that they name: `fold_partner`: column i's fold partner lies in the block of 68 columns with block index (8 - (i div 68)) mod (8); within one block the partners are distinct.
All inputs are finite; a program needn't handle non-finite values.
Results may differ from a plain program's by a relative error of at most 0.0003.
Values sent between devices are 32-bit elements; how exact they have to be, the bound alone decides.
A program may use at most 64 MiB of HBM per device.

v0:
```python
import jax
import jax.numpy as jnp
from jax import lax
from jax.sharding import PartitionSpec as P

PASSES = 4


def extended_2(block, sides, width, periodic):
    for axis, dim in sides:
        count = lax.axis_size(axis)
        forward = [(i, i + 1) for i in range(count - 1)]
        if periodic:
            forward.append((count - 1, 0))
        backward = [(target, source) for source, target in forward]
        low = lax.ppermute(
            lax.slice_in_dim(block, block.shape[dim] - width, None, axis=dim), axis, forward
        )
        high = lax.ppermute(lax.slice_in_dim(block, 0, width, axis=dim), axis, backward)
        block = jnp.concatenate([low, block, high], axis=dim)
    return block


def conductances(coefficients, level_values):
    kappa_padded = coefficients[0]
    wet_padded = (level_values < coefficients[1][None]).astype(jnp.float32)
    row_kappa = kappa_padded[:, 1:-1]
    row_wet = wet_padded[:, :, 1:-1]
    along_lon = (row_kappa[:-1] * row_kappa[1:])[None] * row_wet[:, :-1] * row_wet[:, 1:]
    column_kappa = kappa_padded[1:-1]
    column_wet = wet_padded[:, 1:-1]
    along_lat = (
        (column_kappa[:, :-1] * column_kappa[:, 1:])[None]
        * column_wet[:, :, :-1]
        * column_wet[:, :, 1:]
    )
    return (along_lon[:, 1:], along_lon[:, :-1], along_lat[:, :, 1:], along_lat[:, :, :-1])


def diffuse_once(padded, faces, levels_count):
    east_face, west_face, north_face, south_face = faces
    grid = padded.reshape(2, levels_count, padded.shape[1], padded.shape[2])
    centre = grid[:, :, 1:-1, 1:-1]
    result = (
        centre
        + east_face * (grid[:, :, 2:, 1:-1] - centre)
        + west_face * (grid[:, :, :-2, 1:-1] - centre)
        + north_face * (grid[:, :, 1:-1, 2:] - centre)
        + south_face * (grid[:, :, 1:-1, :-2] - centre)
    )
    return result.reshape(2 * levels_count, padded.shape[1] - 2, padded.shape[2] - 2)


def local(
    control_fields,
    unexplained_elevation,
    diffusivity,
    depth_levels,
    fold_partner,
    prior_sigmas,
    haline_thermal_ratio,
    expansion_coefficients,
):
    levels_count = control_fields.shape[1]
    lon_cells = control_fields.shape[2]
    lat_cells = control_fields.shape[3]
    stacked_rows = 2 * levels_count
    lat_devices = lax.axis_size("lat")
    lon_place = lax.axis_index("lon")
    at_top = (lax.axis_index("lat") == lat_devices - 1).astype(jnp.float32)
    depth_float = depth_levels.astype(jnp.float32)
    level_values = jnp.arange(levels_count, dtype=jnp.float32)[:, None, None]
    wet_cells = (level_values < depth_float[None]).astype(jnp.float32)
    masked = (control_fields * wet_cells[None]).reshape(stacked_rows, lon_cells, lat_cells)
    current = jnp.concatenate([masked, diffusivity[None], depth_float[None]], axis=0)
    margin = 1
    own_columns = lon_place * lon_cells + jnp.arange(lon_cells, dtype=jnp.int32)
    own_partners = fold_partner[own_columns]
    faces = None
    for repeat in range(PASSES):
        extended = extended_2(current, (("lon", 1),), 1, True)
        top_rows = extended[:, margin : margin + lon_cells, lat_cells - 1]
        every_top = lax.all_gather(top_rows, "lon", axis=1, tiled=True)
        folded = jnp.take(every_top, own_partners, axis=1)
        folded = jnp.concatenate(
            [jnp.zeros_like(folded[:, :1]), folded, jnp.zeros_like(folded[:, :1])], axis=1
        )
        padded = extended_2(extended, (("lat", 2),), 1, False)
        padded = padded.at[:, :, lat_cells + 1].add(at_top * folded)
        if repeat == 0:
            faces = conductances(padded[stacked_rows:], level_values)
            padded = padded[:stacked_rows]
            extended = extended[:stacked_rows]
        inner = diffuse_once(padded, faces, levels_count)
        current = inner
    assembled_output = current
    assembled_output = assembled_output.reshape(2, levels_count, lon_cells, lat_cells)
    thermal_grid = prior_sigmas[0][:, None, None] * assembled_output[0]
    saltiness_grid = (
        prior_sigmas[1][:, None, None] * assembled_output[1]
        + haline_thermal_ratio[None] * thermal_grid
    )
    ocean_elevation = unexplained_elevation + jnp.sum(
        expansion_coefficients[0][:, None, None] * thermal_grid
        + expansion_coefficients[1][:, None, None] * saltiness_grid,
        axis=0,
    )
    return (jnp.stack([thermal_grid, saltiness_grid]), ocean_elevation)


def solution(mesh):
    return jax.shard_map(
        local,
        mesh=mesh,
        in_specs=(
            P(None, None, "lon", "lat"),
            P("lon", "lat"),
            P("lon", "lat"),
            P("lon", "lat"),
            P(),
            P(),
            P("lon", "lat"),
            P(),
        ),
        out_specs=(P(None, None, "lon", "lat"), P("lon", "lat")),
        check_vma=False,
    )
```

profile of v0, /device:TPU:1, one launch (start us, length us, event | category | flops | bytes accessed | tf_op | source)
XLA Modules:
  0.0 226.4 jit_solution(13621705072636186898)
XLA Ops:
  3.1 2.1 collective-permute-start
  5.2 3.1 %collective-permute-start.1 = (f32[10,1,384]{2,1,0:T(1,128)S(1)}, f32[10,1,384]{2,1,0:T(1,128)S(1)}, u32[]{:S(2)}, u32[]{:S(2)}) collective-permute-start(f32[10,1,384]{2,1,0:T(1,128)S(1)} %get-tuple-element.74), channel_id=1, source_target_pairs={{4,0},{8,4},{12,8},{16,12},{20,16},{24,20},{28,24},{0,28},{5,1},{9... | collective-permute-start | bytes 46088 | tf_op jit(solution)/shard_map/ppermute | solution.py:19
  10.0 24.6 %all-gather = f32[10,544,1]{0,2,1:T(1,128)S(1)} all-gather(f32[10,68,1]{0,2,1:T(1,128)S(1)} %copy.175), channel_id=2, replica_groups=mesh['lon'=8,'lat'=4] {'lon'}, dimensions={1}, use_global_device_ids=true | all-gather | bytes 24480 | tf_op jit(solution)/shard_map/all_gather | solution.py:83
  35.7 9.0 %collective-permute-start.3 = (f32[10,70,1]{1,2,0:T(1,128)S(1)}, f32[10,70,1]{1,2,0:T(1,128)S(1)}, u32[]{:S(2)}, u32[]{:S(2)}) collective-permute-start(f32[10,70,1]{1,2,0:T(1,128)S(1)} %copy.174), channel_id=1, source_target_pairs={{1,0},{2,1},{3,2},{5,4},{6,5},{7,6},{9,8},{10,9},{11,10},{13,12},{... | collective-permute-start | bytes 8408 | tf_op jit(solution)/shard_map/ppermute | solution.py:19
  44.8 3.3 %collective-permute-start.2 = (f32[10,70,1]{2,1,0:T(8,128)S(1)}, f32[10,70,1]{2,1,0:T(8,128)}, u32[]{:S(2)}, u32[]{:S(2)}) collective-permute-start(f32[10,70,1]{2,1,0:T(8,128)S(1)} %get-tuple-element.71), channel_id=1, source_target_pairs={{0,1},{1,2},{2,3},{4,5},{5,6},{6,7},{8,9},{9,10},{10,11},{12,13},{... | collective-permute-start | bytes 8408 | tf_op jit(solution)/shard_map/ppermute | solution.py:16
  48.7 3.9 %collective-permute-done.2 = f32[10,70,1]{2,1,0:T(8,128)} collective-permute-done((f32[10,70,1]{2,1,0:T(8,128)S(1)}, f32[10,70,1]{2,1,0:T(8,128)}, u32[]{:S(2)}, u32[]{:S(2)}) %collective-permute-start.2) | collective-permute-done | bytes 2832 | tf_op jit(solution)/shard_map/ppermute | solution.py:16
  54.2 3.6 %scatter-add.14 = f32[10,70,386]{2,1,0:T(8,128)S(1)} dynamic-update-slice(f32[10,70,386]{2,1,0:T(8,128)S(1)} %pad_maximum_fusion.3, f32[10,70,1]{2,1,0:T(8,128)S(1)} %copy.148, s32[]{:T(128)} %constant.128.clone.1, s32[]{:T(128)} %constant.128.clone.1, s32[]{:T(128)} %constant.132.clone.1) | dynamic-update-slice | bytes 5604 | tf_op jit(solution)/shard_map/scatter-add | solution.py:89
  63.2 24.8 %all-gather.1 = f32[8,544,1]{0,2,1:T(1,128)S(1)} all-gather(f32[8,68,1]{0,2,1:T(1,128)S(1)} %copy.154), channel_id=3, replica_groups=mesh['lon'=8,'lat'=4] {'lon'}, dimensions={1}, use_global_device_ids=true | all-gather | bytes 19584 | tf_op jit(solution)/shard_map/all_gather | solution.py:83
  91.6 11.1 %collective-permute-start.6 = (f32[8,70,1]{1,0,2:T(8,128)S(1)}, f32[8,70,1]{1,0,2:T(8,128)S(1)}, u32[]{:S(2)}, u32[]{:S(2)}) collective-permute-start(f32[8,70,1]{1,0,2:T(8,128)S(1)} %get-tuple-element.67), channel_id=1, source_target_pairs={{0,1},{1,2},{2,3},{4,5},{5,6},{6,7},{8,9},{9,10},{10,11},{12,13},{... | collective-permute-start | bytes 6728 | tf_op jit(solution)/shard_map/ppermute | solution.py:16
  102.8 1.9 collective-permute-start.7
  104.8 2.8 %collective-permute-done.7 = f32[8,70,1]{1,0,2:T(8,128)S(1)} collective-permute-done((f32[8,70,1]{1,0,2:T(8,128)S(1)}, f32[8,70,1]{1,0,2:T(8,128)S(1)}, u32[]{:S(2)}, u32[]{:S(2)}) %collective-permute-start.7) | collective-permute-done | bytes 2272 | tf_op jit(solution)/shard_map/ppermute | solution.py:19
  107.7 3.5 %pad_maximum_fusion = f32[8,70,386]{1,0,2:T(8,128)} fusion(f32[8,70,1]{1,0,2:T(8,128)S(1)} %collective-permute-done.7, f32[8,1,384]{1,0,2:T(8,128)} %copy.153, f32[8,68,384]{1,0,2:T(8,128)S(1)} %copy.152, f32[8,1,384]{1,0,2:T(8,128)S(1)} %copy.151, f32[8,70,1]{1,0,2:T(8,128)S(1)} %collective-permute-done.6), kind=kLoop, calls=%fused_computation.5 | loop fusion | flops 864640 | bytes 1729280 | tf_op jit(solution)/shard_map/concatenate | solution.py:20
  111.8 2.1 copy.156
  116.5 2.8 %collective-permute-start.9 = (f32[8,1,384]{2,0,1:T(8,128)S(1)}, f32[8,1,384]{2,0,1:T(8,128)S(1)}, u32[]{:S(2)}, u32[]{:S(2)}) collective-permute-start(f32[8,1,384]{2,0,1:T(8,128)S(1)} %copy.158), channel_id=1, source_target_pairs={{4,0},{8,4},{12,8},{16,12},{20,16},{24,20},{28,24},{0,28},{5,1},{9... | collective-permute-start | bytes 36872 | tf_op jit(solution)/shard_map/ppermute | solution.py:19
  121.7 25.0 %all-gather.2 = f32[8,544,1]{0,2,1:T(1,128)S(1)} all-gather(f32[8,68,1]{0,2,1:T(1,128)S(1)} %copy.162), channel_id=4, replica_groups=mesh['lon'=8,'lat'=4] {'lon'}, dimensions={1}, use_global_device_ids=true | all-gather | bytes 19584 | tf_op jit(solution)/shard_map/all_gather | solution.py:83
  150.4 8.4 %collective-permute-start.10 = (f32[8,70,1]{1,0,2:T(8,128)S(1)}, f32[8,70,1]{1,0,2:T(8,128)S(1)}, u32[]{:S(2)}, u32[]{:S(2)}) collective-permute-start(f32[8,70,1]{1,0,2:T(8,128)S(1)} %get-tuple-element.65), channel_id=1, source_target_pairs={{0,1},{1,2},{2,3},{4,5},{5,6},{6,7},{8,9},{9,10},{10,11},{12,13},{... | collective-permute-start | bytes 6728 | tf_op jit(solution)/shard_map/ppermute | solution.py:16
  160.9 2.8 %collective-permute-done.11 = f32[8,70,1]{1,0,2:T(8,128)S(1)} collective-permute-done((f32[8,70,1]{1,0,2:T(8,128)S(1)}, f32[8,70,1]{1,0,2:T(8,128)S(1)}, u32[]{:S(2)}, u32[]{:S(2)}) %collective-permute-start.11) | collective-permute-done | bytes 2272 | tf_op jit(solution)/shard_map/ppermute | solution.py:19
  163.7 3.5 %pad_maximum_fusion.1 = f32[8,70,386]{1,0,2:T(8,128)} fusion(f32[8,70,1]{1,0,2:T(8,128)S(1)} %collective-permute-done.11, f32[8,1,384]{1,0,2:T(8,128)} %copy.161, f32[8,68,384]{1,0,2:T(8,128)S(1)} %copy.160, f32[8,1,384]{1,0,2:T(8,128)S(1)} %copy.159, f32[8,70,1]{1,0,2:T(8,128)S(1)} %collective-permute-done.10), kind=kLoop, calls=%fused_computation.6 | loop fusion | flops 864640 | bytes 1729280 | tf_op jit(solution)/shard_map/concatenate | solution.py:20
  167.9 2.1 copy.164
  175.0 24.9 %all-gather.3 = f32[8,544,1]{0,2,1:T(1,128)S(1)} all-gather(f32[8,68,1]{0,2,1:T(1,128)S(1)} %copy.170), channel_id=5, replica_groups=mesh['lon'=8,'lat'=4] {'lon'}, dimensions={1}, use_global_device_ids=true | all-gather | bytes 19584 | tf_op jit(solution)/shard_map/all_gather | solution.py:83
  203.6 8.4 %collective-permute-start.14 = (f32[8,70,1]{1,0,2:T(8,128)S(1)}, f32[8,70,1]{1,0,2:T(8,128)S(1)}, u32[]{:S(2)}, u32[]{:S(2)}) collective-permute-start(f32[8,70,1]{1,0,2:T(8,128)S(1)} %get-tuple-element.63), channel_id=1, source_target_pairs={{0,1},{1,2},{2,3},{4,5},{5,6},{6,7},{8,9},{9,10},{10,11},{12,13},{... | collective-permute-start | bytes 6728 | tf_op jit(solution)/shard_map/ppermute | solution.py:16
  214.1 2.8 %collective-permute-done.15 = f32[8,70,1]{1,0,2:T(8,128)S(1)} collective-permute-done((f32[8,70,1]{1,0,2:T(8,128)S(1)}, f32[8,70,1]{1,0,2:T(8,128)S(1)}, u32[]{:S(2)}, u32[]{:S(2)}) %collective-permute-start.15) | collective-permute-done | bytes 2272 | tf_op jit(solution)/shard_map/ppermute | solution.py:19
  216.9 3.5 %pad_maximum_fusion.2 = f32[8,70,386]{1,0,2:T(8,128)} fusion(f32[8,70,1]{1,0,2:T(8,128)S(1)} %collective-permute-done.15, f32[8,1,384]{1,0,2:T(8,128)} %copy.169, f32[8,68,384]{1,0,2:T(8,128)S(1)} %copy.168, f32[8,1,384]{1,0,2:T(8,128)S(1)} %copy.167, f32[8,70,1]{1,0,2:T(8,128)S(1)} %collective-permute-done.14), kind=kLoop, calls=%fused_computation.7 | loop fusion | flops 864640 | bytes 1729280 | tf_op jit(solution)/shard_map/concatenate | solution.py:20
  221.1 2.1 copy.172
  (151 shorter events, 42.9 us)
Async XLA Ops:
  0.6 7.7 %copy-start = (s32[544]{0:T(1024)S(1)}, s32[544]{0:T(1024)}, u32[]{:S(2)}) copy-start(s32[544]{0:T(1024)} %param.22) | copy-start | bytes 6532
  3.1 32.2 %collective-permute-start = (f32[10,1,384]{2,1,0:T(1,128)S(1)}, f32[10,1,384]{2,1,0:T(1,128)S(1)}, u32[]{:S(2)}, u32[]{:S(2)}) collective-permute-start(f32[10,1,384]{2,1,0:T(1,128)S(1)} %get-tuple-element.73), channel_id=1, source_target_pairs={{0,4},{4,8},{8,12},{12,16},{16,20},{20,24},{24,28},{28,0},{1,5},{5... | collective-permute-start | bytes 46088 | tf_op jit(solution)/shard_map/ppermute | solution.py:16
  5.2 30.1 %collective-permute-start.1 = (f32[10,1,384]{2,1,0:T(1,128)S(1)}, f32[10,1,384]{2,1,0:T(1,128)S(1)}, u32[]{:S(2)}, u32[]{:S(2)}) collective-permute-start(f32[10,1,384]{2,1,0:T(1,128)S(1)} %get-tuple-element.74), channel_id=1, source_target_pairs={{4,0},{8,4},{12,8},{16,12},{20,16},{24,20},{28,24},{0,28},{5,1},{9... | collective-permute-start | bytes 46088 | tf_op jit(solution)/shard_map/ppermute | solution.py:19
  35.7 12.4 %collective-permute-start.3 = (f32[10,70,1]{1,2,0:T(1,128)S(1)}, f32[10,70,1]{1,2,0:T(1,128)S(1)}, u32[]{:S(2)}, u32[]{:S(2)}) collective-permute-start(f32[10,70,1]{1,2,0:T(1,128)S(1)} %copy.174), channel_id=1, source_target_pairs={{1,0},{2,1},{3,2},{5,4},{6,5},{7,6},{9,8},{10,9},{11,10},{13,12},{... | collective-permute-start | bytes 8408 | tf_op jit(solution)/shard_map/ppermute | solution.py:19
  44.8 7.7 %collective-permute-start.2 = (f32[10,70,1]{2,1,0:T(8,128)S(1)}, f32[10,70,1]{2,1,0:T(8,128)}, u32[]{:S(2)}, u32[]{:S(2)}) collective-permute-start(f32[10,70,1]{2,1,0:T(8,128)S(1)} %get-tuple-element.71), channel_id=1, source_target_pairs={{0,1},{1,2},{2,3},{4,5},{5,6},{6,7},{8,9},{9,10},{10,11},{12,13},{... | collective-permute-start | bytes 8408 | tf_op jit(solution)/shard_map/ppermute | solution.py:16
  60.4 28.8 %collective-permute-start.5 = (f32[8,1,384]{2,0,1:T(8,128)S(1)}, f32[8,1,384]{2,0,1:T(8,128)S(1)}, u32[]{:S(2)}, u32[]{:S(2)}) collective-permute-start(f32[8,1,384]{2,0,1:T(8,128)S(1)} %copy.150), channel_id=1, source_target_pairs={{4,0},{8,4},{12,8},{16,12},{20,16},{24,20},{28,24},{0,28},{5,1},{9... | collective-permute-start | bytes 36872 | tf_op jit(solution)/shard_map/ppermute | solution.py:19
  61.9 26.7 %collective-permute-start.4 = (f32[8,1,384]{2,0,1:T(8,128)S(1)}, f32[8,1,384]{2,0,1:T(8,128)S(1)}, u32[]{:S(2)}, u32[]{:S(2)}) collective-permute-start(f32[8,1,384]{2,0,1:T(8,128)S(1)} %copy.149), channel_id=1, source_target_pairs={{0,4},{4,8},{8,12},{12,16},{16,20},{20,24},{24,28},{28,0},{1,5},{5... | collective-permute-start | bytes 36872 | tf_op jit(solution)/shard_map/ppermute | solution.py:16
  91.6 13.2 %collective-permute-start.6 = (f32[8,70,1]{1,0,2:T(8,128)S(1)}, f32[8,70,1]{1,0,2:T(8,128)S(1)}, u32[]{:S(2)}, u32[]{:S(2)}) collective-permute-start(f32[8,70,1]{1,0,2:T(8,128)S(1)} %get-tuple-element.67), channel_id=1, source_target_pairs={{0,1},{1,2},{2,3},{4,5},{5,6},{6,7},{8,9},{9,10},{10,11},{12,13},{... | collective-permute-start | bytes 6728 | tf_op jit(solution)/shard_map/ppermute | solution.py:16
  102.8 4.9 %collective-permute-start.7 = (f32[8,70,1]{1,0,2:T(8,128)S(1)}, f32[8,70,1]{1,0,2:T(8,128)S(1)}, u32[]{:S(2)}, u32[]{:S(2)}) collective-permute-start(f32[8,70,1]{1,0,2:T(8,128)S(1)} %get-tuple-element.68), channel_id=1, source_target_pairs={{1,0},{2,1},{3,2},{5,4},{6,5},{7,6},{9,8},{10,9},{11,10},{13,12},{... | collective-permute-start | bytes 6728 | tf_op jit(solution)/shard_map/ppermute | solution.py:19
  111.2 2.8 %copy-start.2 = (f32[4,68,384]{2,1,0:T(8,128)S(1)}, f32[4,68,384]{2,1,0:T(8,128)}, u32[]{:S(2)}) copy-start(f32[4,68,384]{2,1,0:T(8,128)} %copy-done.1) | copy-start | bytes 1253380
  111.2 2.8 %copy-start.6 = (f32[4,68,384]{2,1,0:T(8,128)S(1)}, f32[4,68,384]{2,1,0:T(8,128)}, u32[]{:S(2)}) copy-start(f32[4,68,384]{2,1,0:T(8,128)} %copy-done.5) | copy-start | bytes 1253380
  111.2 2.8 %copy-start.10 = (f32[4,68,384]{2,1,0:T(8,128)S(1)}, f32[4,68,384]{2,1,0:T(8,128)}, u32[]{:S(2)}) copy-start(f32[4,68,384]{2,1,0:T(8,128)} %copy-done.9) | copy-start | bytes 1253380
  111.2 2.8 %copy-start.14 = (f32[4,68,384]{2,1,0:T(8,128)S(1)}, f32[4,68,384]{2,1,0:T(8,128)}, u32[]{:S(2)}) copy-start(f32[4,68,384]{2,1,0:T(8,128)} %copy-done.13) | copy-start | bytes 1253380
  115.0 4.3 %copy-start.18 = (f32[2,4,68,384]{3,2,1,0:T(8,128)}, f32[2,4,68,384]{3,2,1,0:T(8,128)S(1)}, u32[]{:S(2)}) copy-start(f32[2,4,68,384]{3,2,1,0:T(8,128)S(1)} %fusion.17) | copy-start | bytes 2506756
  115.0 32.3 %collective-permute-start.8 = (f32[8,1,384]{2,0,1:T(8,128)S(1)}, f32[8,1,384]{2,0,1:T(8,128)S(1)}, u32[]{:S(2)}, u32[]{:S(2)}) collective-permute-start(f32[8,1,384]{2,0,1:T(8,128)S(1)} %copy.157), channel_id=1, source_target_pairs={{0,4},{4,8},{8,12},{12,16},{16,20},{20,24},{24,28},{28,0},{1,5},{5... | collective-permute-start | bytes 36872 | tf_op jit(solution)/shard_map/ppermute | solution.py:16
  116.5 31.4 %collective-permute-start.9 = (f32[8,1,384]{2,0,1:T(8,128)S(1)}, f32[8,1,384]{2,0,1:T(8,128)S(1)}, u32[]{:S(2)}, u32[]{:S(2)}) collective-permute-start(f32[8,1,384]{2,0,1:T(8,128)S(1)} %copy.158), channel_id=1, source_target_pairs={{4,0},{8,4},{12,8},{16,12},{20,16},{24,20},{28,24},{0,28},{5,1},{9... | collective-permute-start | bytes 36872 | tf_op jit(solution)/shard_map/ppermute | solution.py:19
  150.4 10.5 %collective-permute-start.10 = (f32[8,70,1]{1,0,2:T(8,128)S(1)}, f32[8,70,1]{1,0,2:T(8,128)S(1)}, u32[]{:S(2)}, u32[]{:S(2)}) collective-permute-start(f32[8,70,1]{1,0,2:T(8,128)S(1)} %get-tuple-element.65), channel_id=1, source_target_pairs={{0,1},{1,2},{2,3},{4,5},{5,6},{6,7},{8,9},{9,10},{10,11},{12,13},{... | collective-permute-start | bytes 6728 | tf_op jit(solution)/shard_map/ppermute | solution.py:16
  158.8 4.9 %collective-permute-start.11 = (f32[8,70,1]{1,0,2:T(8,128)S(1)}, f32[8,70,1]{1,0,2:T(8,128)S(1)}, u32[]{:S(2)}, u32[]{:S(2)}) collective-permute-start(f32[8,70,1]{1,0,2:T(8,128)S(1)} %get-tuple-element.66), channel_id=1, source_target_pairs={{1,0},{2,1},{3,2},{5,4},{6,5},{7,6},{9,8},{10,9},{11,10},{13,12},{... | collective-permute-start | bytes 6728 | tf_op jit(solution)/shard_map/ppermute | solution.py:19
  167.2 2.8 %copy-start.15 = (f32[4,68,384]{2,1,0:T(8,128)S(1)}, f32[4,68,384]{2,1,0:T(8,128)}, u32[]{:S(2)}) copy-start(f32[4,68,384]{2,1,0:T(8,128)} %copy-done.13) | copy-start | bytes 1253380
  171.1 30.1 %collective-permute-start.13 = (f32[8,1,384]{2,0,1:T(8,128)S(1)}, f32[8,1,384]{2,0,1:T(8,128)S(1)}, u32[]{:S(2)}, u32[]{:S(2)}) collective-permute-start(f32[8,1,384]{2,0,1:T(8,128)S(1)} %copy.166), channel_id=1, source_target_pairs={{4,0},{8,4},{12,8},{16,12},{20,16},{24,20},{28,24},{0,28},{5,1},{9... | collective-permute-start | bytes 36872 | tf_op jit(solution)/shard_map/ppermute | solution.py:19
  172.6 28.0 %collective-permute-start.12 = (f32[8,1,384]{2,0,1:T(8,128)S(1)}, f32[8,1,384]{2,0,1:T(8,128)S(1)}, u32[]{:S(2)}, u32[]{:S(2)}) collective-permute-start(f32[8,1,384]{2,0,1:T(8,128)S(1)} %copy.165), channel_id=1, source_target_pairs={{0,4},{4,8},{8,12},{12,16},{16,20},{20,24},{24,28},{28,0},{1,5},{5... | collective-permute-start | bytes 36872 | tf_op jit(solution)/shard_map/ppermute | solution.py:16
  203.6 10.5 %collective-permute-start.14 = (f32[8,70,1]{1,0,2:T(8,128)S(1)}, f32[8,70,1]{1,0,2:T(8,128)S(1)}, u32[]{:S(2)}, u32[]{:S(2)}) collective-permute-start(f32[8,70,1]{1,0,2:T(8,128)S(1)} %get-tuple-element.63), channel_id=1, source_target_pairs={{0,1},{1,2},{2,3},{4,5},{5,6},{6,7},{8,9},{9,10},{10,11},{12,13},{... | collective-permute-start | bytes 6728 | tf_op jit(solution)/shard_map/ppermute | solution.py:16
  212.0 4.9 %collective-permute-start.15 = (f32[8,70,1]{1,0,2:T(8,128)S(1)}, f32[8,70,1]{1,0,2:T(8,128)S(1)}, u32[]{:S(2)}, u32[]{:S(2)}) collective-permute-start(f32[8,70,1]{1,0,2:T(8,128)S(1)} %get-tuple-element.64), channel_id=1, source_target_pairs={{1,0},{2,1},{3,2},{5,4},{6,5},{7,6},{9,8},{10,9},{11,10},{13,12},{... | collective-permute-start | bytes 6728 | tf_op jit(solution)/shard_map/ppermute | solution.py:19
  220.4 2.8 %copy-start.16 = (f32[4,68,384]{2,1,0:T(8,128)S(1)}, f32[4,68,384]{2,1,0:T(8,128)}, u32[]{:S(2)}) copy-start(f32[4,68,384]{2,1,0:T(8,128)} %copy-done.13) | copy-start | bytes 1253380
  (16 other events, 31.5 us)
where the time goes:
time: 227 us; the launch traced here: 226 us
  blocking collectives  99.3 us (44%)
  starting transfers between devices  58.5 us (26%)
  local copies, waits for them, and re-layouts  29.4 us (13%)
  other arithmetic  25.4 us (11%)
  waiting for transfers between devices  12.4 us (5%)
    all_gather x4, blocking collectives, local(): every_top = lax.all_gather(top_rows, 'lon', axis=1, tiled=True)  99.3 us
    ppermute x8, starting transfers between devices, extended_2(): lax.ppermute(lax.slice_in_dim(block, block.shape[dim] - width, None, axis...  34.8 us
    ppermute x8, starting transfers between devices, extended_2(): lax.ppermute(lax.slice_in_dim(block, 0, width, axis=dim), axis, backward)  23.7 us
    concatenate x4, other arithmetic, extended_2(): block = jnp.concatenate([low, block, high], axis=dim)  12.1 us
    scatter-add x4, local copies, waits for them, and re-layouts, local(): padded = padded.at[:, :, lat_cells + 1].add(at_top * folded)  9.92 us
    ppermute x8, waiting for transfers between devices, extended_2(): lax.ppermute(lax.slice_in_dim(block, 0, width, axis=dim), axis, backward)  8.54 us
    ppermute x4, local copies, waits for them, and re-layouts, extended_2(): lax.ppermute(lax.slice_in_dim(block, 0, width, axis=dim), axis, backward)  5.23 us
  transfers between devices with their start and end apart: 16, of which 4 were waited for; matrix products, arithmetic and copies ran while one was open for 6% of the time, Pallas kernels for 0%

commit v1 on v0

--- a/solution.py
+++ b/solution.py
@@ -80,7 +80,14 @@
     for repeat in range(PASSES):
         extended = extended_2(current, (("lon", 1),), 1, True)
         top_rows = extended[:, margin : margin + lon_cells, lat_cells - 1]
-        every_top = lax.all_gather(top_rows, "lon", axis=1, tiled=True)
+        ring = [top_rows]
+        for hop in range(7):
+            ring.append(lax.ppermute(ring[-1], "lon", [(dev, (dev + 1) % 8) for dev in range(8)]))
+        every_top = jnp.roll(
+            jnp.concatenate(ring[::-1], axis=1),
+            (lax.axis_index("lon") + 1) * ring[0].shape[1],
+            axis=1,
+        )
         folded = jnp.take(every_top, own_partners, axis=1)
         folded = jnp.concatenate(
             [jnp.zeros_like(folded[:, :1]), folded, jnp.zeros_like(folded[:, :1])], axis=1

time: 227 us -> 224 us (0.987)
  blocking collectives: 99.3 us -> 0 us
  waiting for transfers between devices: 12.4 us -> 104 us
  starting transfers between devices: 58.5 us -> 68.1 us
  other arithmetic: 25.4 us -> 20.7 us
    all_gather x4 -> x0, blocking collectives: 99.3 us -> none  [local(): every_top = lax.all_gather(top_rows, 'lon', axis=1, tiled=True)]
    ppermute x0 -> x28, waiting for transfers between devices: none -> 90.5 us  [local(): lax.ppermute(ring[-1], 'lon', [(dev, (dev + 1) % 8) for dev in range(8)])]
    ppermute x8, starting transfers between devices: 23.7 us -> 29.2 us  [extended_2(): lax.ppermute(lax.slice_in_dim(block, 0, width, axis=dim), axis, backward)]
    concatenate x4, other arithmetic: 12.1 us -> 6.77 us  [extended_2(): block = jnp.concatenate([low, block, high], axis=dim)]
    ppermute x0 -> x28, starting transfers between devices: none -> 2.53 us  [local(): lax.ppermute(ring[-1], 'lon', [(dev, (dev + 1) % 8) for dev in range(8)])]
  transfers between devices with their start and end apart: 16 -> 44, of which waited for: 4 -> 27; matrix products, arithmetic and copies ran while one was open for 6% -> 10% of each run, Pallas kernels for 0% -> 0%
where the time goes in v1:
time: 224 us; the launch traced here: 223 us
  waiting for transfers between devices  104 us (46%)
  starting transfers between devices  68.1 us (30%)
  local copies, waits for them, and re-layouts  29.3 us (13%)
  other arithmetic  20.7 us (9%)
    ppermute x28, waiting for transfers between devices, local(): lax.ppermute(ring[-1], 'lon', [(dev, (dev + 1) % 8) for dev in range(8)])  90.5 us
    ppermute x8, starting transfers between devices, extended_2(): lax.ppermute(lax.slice_in_dim(block, block.shape[dim] - width, None, axis...  36.3 us
    ppermute x8, starting transfers between devices, extended_2(): lax.ppermute(lax.slice_in_dim(block, 0, width, axis=dim), axis, backward)  29.2 us
    scatter-add x4, local copies, waits for them, and re-layouts, local(): padded = padded.at[:, :, lat_cells + 1].add(at_top * folded)  9.92 us
    ppermute x8, waiting for transfers between devices, extended_2(): lax.ppermute(lax.slice_in_dim(block, 0, width, axis=dim), axis, backward)  8.99 us
    concatenate x4, other arithmetic, extended_2(): block = jnp.concatenate([low, block, high], axis=dim)  6.77 us
    ppermute x4, local copies, waits for them, and re-layouts, extended_2(): lax.ppermute(lax.slice_in_dim(block, 0, width, axis=dim), axis, backward)  5.19 us
  transfers between devices with their start and end apart: 44, of which 27 were waited for; matrix products, arithmetic and copies ran while one was open for 10% of the time, Pallas kernels for 0%

profile of v1, /device:TPU:1, one launch (start us, length us, event | category | flops | bytes accessed | tf_op | source)
XLA Modules:
  0.0 223.3 jit_solution(1231210806769968199)
XLA Ops:
  9.8 5.2 %collective-permute-done.5 = f32[10,68]{1,0:T(8,128)S(1)} collective-permute-done((f32[10,68]{1,0:T(8,128)S(1)}, f32[10,68]{1,0:T(8,128)S(1)}, u32[]{:S(2)}, u32[]{:S(2)}) %collective-permute-start.5) | collective-permute-done | bytes 2752 | tf_op jit(solution)/shard_map/ppermute | solution.py:85
  16.0 4.2 %collective-permute-done.6 = f32[10,68]{1,0:T(8,128)S(1)} collective-permute-done((f32[10,68]{1,0:T(8,128)S(1)}, f32[10,68]{1,0:T(8,128)S(1)}, u32[]{:S(2)}, u32[]{:S(2)}) %collective-permute-start.6) | collective-permute-done | bytes 2752 | tf_op jit(solution)/shard_map/ppermute | solution.py:85
  20.2 5.2 %collective-permute-done.7 = f32[10,68]{1,0:T(8,128)S(1)} collective-permute-done((f32[10,68]{1,0:T(8,128)S(1)}, f32[10,68]{1,0:T(8,128)S(1)}, u32[]{:S(2)}, u32[]{:S(2)}) %collective-permute-start.7) | collective-permute-done | bytes 2752 | tf_op jit(solution)/shard_map/ppermute | solution.py:85
  25.4 5.2 %collective-permute-done.8 = f32[10,68]{1,0:T(8,128)S(1)} collective-permute-done((f32[10,68]{1,0:T(8,128)S(1)}, f32[10,68]{1,0:T(8,128)S(1)}, u32[]{:S(2)}, u32[]{:S(2)}) %collective-permute-start.8) | collective-permute-done | bytes 2752 | tf_op jit(solution)/shard_map/ppermute | solution.py:85
  30.9 8.0 %collective-permute-start.3 = (f32[10,70,1]{1,2,0:T(1,128)S(1)}, f32[10,70,1]{1,2,0:T(1,128)S(1)}, u32[]{:S(2)}, u32[]{:S(2)}) collective-permute-start(f32[10,70,1]{1,2,0:T(1,128)S(1)} %copy.214), channel_id=1, source_target_pairs={{1,0},{2,1},{3,2},{5,4},{6,5},{7,6},{9,8},{10,9},{11,10},{13,12},{... | collective-permute-start | bytes 8408 | tf_op jit(solution)/shard_map/ppermute | solution.py:19
  42.4 4.1 %collective-permute-done.2 = f32[10,70,1]{2,1,0:T(8,128)S(1)} collective-permute-done((f32[10,70,1]{2,1,0:T(8,128)S(1)}, f32[10,70,1]{2,1,0:T(8,128)S(1)}, u32[]{:S(2)}, u32[]{:S(2)}) %collective-permute-start.2) | collective-permute-done | bytes 2832 | tf_op jit(solution)/shard_map/ppermute | solution.py:16
  55.6 5.1 %collective-permute-done.15 = f32[8,68]{1,0:T(8,128)S(1)} collective-permute-done((f32[8,68]{1,0:T(8,128)S(1)}, f32[8,68]{1,0:T(8,128)S(1)}, u32[]{:S(2)}, u32[]{:S(2)}) %collective-permute-start.15) | collective-permute-done | bytes 2208 | tf_op jit(solution)/shard_map/ppermute | solution.py:85
  60.8 5.2 %collective-permute-done.16 = f32[8,68]{1,0:T(8,128)S(1)} collective-permute-done((f32[8,68]{1,0:T(8,128)S(1)}, f32[8,68]{1,0:T(8,128)S(1)}, u32[]{:S(2)}, u32[]{:S(2)}) %collective-permute-start.16) | collective-permute-done | bytes 2208 | tf_op jit(solution)/shard_map/ppermute | solution.py:85
  65.9 5.2 %collective-permute-done.17 = f32[8,68]{1,0:T(8,128)S(1)} collective-permute-done((f32[8,68]{1,0:T(8,128)S(1)}, f32[8,68]{1,0:T(8,128)S(1)}, u32[]{:S(2)}, u32[]{:S(2)}) %collective-permute-start.17) | collective-permute-done | bytes 2208 | tf_op jit(solution)/shard_map/ppermute | solution.py:85
  71.2 4.2 %collective-permute-start.12 = (f32[8,1,384]{2,0,1:T(8,128)S(1)}, f32[8,1,384]{2,0,1:T(8,128)S(1)}, u32[]{:S(2)}, u32[]{:S(2)}) collective-permute-start(f32[8,1,384]{2,0,1:T(8,128)S(1)} %copy.190), channel_id=1, source_target_pairs={{4,0},{8,4},{12,8},{16,12},{20,16},{24,20},{28,24},{0,28},{5,1},{9... | collective-permute-start | bytes 36872 | tf_op jit(solution)/shard_map/ppermute | solution.py:19
  76.9 4.5 %collective-permute-done.19 = f32[8,68]{1,0:T(8,128)S(1)} collective-permute-done((f32[8,68]{1,0:T(8,128)S(1)}, f32[8,68]{1,0:T(8,128)S(1)}, u32[]{:S(2)}, u32[]{:S(2)}) %collective-permute-start.19) | collective-permute-done | bytes 2208 | tf_op jit(solution)/shard_map/ppermute | solution.py:85
  84.6 10.5 %collective-permute-start.13 = (f32[8,70,1]{1,0,2:T(8,128)S(1)}, f32[8,70,1]{1,0,2:T(8,128)S(1)}, u32[]{:S(2)}, u32[]{:S(2)}) collective-permute-start(f32[8,70,1]{1,0,2:T(8,128)S(1)} %get-tuple-element.70), channel_id=1, source_target_pairs={{0,1},{1,2},{2,3},{4,5},{5,6},{6,7},{8,9},{9,10},{10,11},{12,13},{... | collective-permute-start | bytes 6728 | tf_op jit(solution)/shard_map/ppermute | solution.py:16
  107.6 4.2 %collective-permute-start.23 = (f32[8,1,384]{2,0,1:T(8,128)S(1)}, f32[8,1,384]{2,0,1:T(8,128)S(1)}, u32[]{:S(2)}, u32[]{:S(2)}) collective-permute-start(f32[8,1,384]{2,0,1:T(8,128)S(1)} %copy.198), channel_id=1, source_target_pairs={{4,0},{8,4},{12,8},{16,12},{20,16},{24,20},{28,24},{0,28},{5,1},{9... | collective-permute-start | bytes 36872 | tf_op jit(solution)/shard_map/ppermute | solution.py:19
  112.2 5.3 %collective-permute-done.26 = f32[8,68]{1,0:T(8,128)S(1)} collective-permute-done((f32[8,68]{1,0:T(8,128)S(1)}, f32[8,68]{1,0:T(8,128)S(1)}, u32[]{:S(2)}, u32[]{:S(2)}) %collective-permute-start.26) | collective-permute-done | bytes 2208 | tf_op jit(solution)/shard_map/ppermute | solution.py:85
  117.5 5.2 %collective-permute-done.27 = f32[8,68]{1,0:T(8,128)S(1)} collective-permute-done((f32[8,68]{1,0:T(8,128)S(1)}, f32[8,68]{1,0:T(8,128)S(1)}, u32[]{:S(2)}, u32[]{:S(2)}) %collective-permute-start.27) | collective-permute-done | bytes 2208 | tf_op jit(solution)/shard_map/ppermute | solution.py:85
  122.7 5.2 %collective-permute-done.28 = f32[8,68]{1,0:T(8,128)S(1)} collective-permute-done((f32[8,68]{1,0:T(8,128)S(1)}, f32[8,68]{1,0:T(8,128)S(1)}, u32[]{:S(2)}, u32[]{:S(2)}) %collective-permute-start.28) | collective-permute-done | bytes 2208 | tf_op jit(solution)/shard_map/ppermute | solution.py:85
  127.8 5.2 %collective-permute-done.29 = f32[8,68]{1,0:T(8,128)S(1)} collective-permute-done((f32[8,68]{1,0:T(8,128)S(1)}, f32[8,68]{1,0:T(8,128)S(1)}, u32[]{:S(2)}, u32[]{:S(2)}) %collective-permute-start.29) | collective-permute-done | bytes 2208 | tf_op jit(solution)/shard_map/ppermute | solution.py:85
  141.3 10.6 %collective-permute-start.24 = (f32[8,70,1]{1,0,2:T(8,128)S(1)}, f32[8,70,1]{1,0,2:T(8,128)S(1)}, u32[]{:S(2)}, u32[]{:S(2)}) collective-permute-start(f32[8,70,1]{1,0,2:T(8,128)S(1)} %get-tuple-element.68), channel_id=1, source_target_pairs={{0,1},{1,2},{2,3},{4,5},{5,6},{6,7},{8,9},{9,10},{10,11},{12,13},{... | collective-permute-start | bytes 6728 | tf_op jit(solution)/shard_map/ppermute | solution.py:16
  164.4 4.1 %collective-permute-start.34 = (f32[8,1,384]{2,0,1:T(8,128)S(1)}, f32[8,1,384]{2,0,1:T(8,128)S(1)}, u32[]{:S(2)}, u32[]{:S(2)}) collective-permute-start(f32[8,1,384]{2,0,1:T(8,128)S(1)} %copy.206), channel_id=1, source_target_pairs={{4,0},{8,4},{12,8},{16,12},{20,16},{24,20},{28,24},{0,28},{5,1},{9... | collective-permute-start | bytes 36872 | tf_op jit(solution)/shard_map/ppermute | solution.py:19
  168.9 5.1 %collective-permute-done.37 = f32[8,68]{1,0:T(8,128)S(1)} collective-permute-done((f32[8,68]{1,0:T(8,128)S(1)}, f32[8,68]{1,0:T(8,128)S(1)}, u32[]{:S(2)}, u32[]{:S(2)}) %collective-permute-start.37) | collective-permute-done | bytes 2208 | tf_op jit(solution)/shard_map/ppermute | solution.py:85
  174.1 5.4 %collective-permute-done.38 = f32[8,68]{1,0:T(8,128)S(1)} collective-permute-done((f32[8,68]{1,0:T(8,128)S(1)}, f32[8,68]{1,0:T(8,128)S(1)}, u32[]{:S(2)}, u32[]{:S(2)}) %collective-permute-start.38) | collective-permute-done | bytes 2208 | tf_op jit(solution)/shard_map/ppermute | solution.py:85
  179.4 5.2 %collective-permute-done.39 = f32[8,68]{1,0:T(8,128)S(1)} collective-permute-done((f32[8,68]{1,0:T(8,128)S(1)}, f32[8,68]{1,0:T(8,128)S(1)}, u32[]{:S(2)}, u32[]{:S(2)}) %collective-permute-start.39) | collective-permute-done | bytes 2208 | tf_op jit(solution)/shard_map/ppermute | solution.py:85
  184.6 5.2 %collective-permute-done.40 = f32[8,68]{1,0:T(8,128)S(1)} collective-permute-done((f32[8,68]{1,0:T(8,128)S(1)}, f32[8,68]{1,0:T(8,128)S(1)}, u32[]{:S(2)}, u32[]{:S(2)}) %collective-permute-start.40) | collective-permute-done | bytes 2208 | tf_op jit(solution)/shard_map/ppermute | solution.py:85
  198.1 10.6 %collective-permute-start.35 = (f32[8,70,1]{1,0,2:T(8,128)S(1)}, f32[8,70,1]{1,0,2:T(8,128)S(1)}, u32[]{:S(2)}, u32[]{:S(2)}) collective-permute-start(f32[8,70,1]{1,0,2:T(8,128)S(1)} %get-tuple-element.66), channel_id=1, source_target_pairs={{0,1},{1,2},{2,3},{4,5},{5,6},{6,7},{8,9},{9,10},{10,11},{12,13},{... | collective-permute-start | bytes 6728 | tf_op jit(solution)/shard_map/ppermute | solution.py:16
  (218 shorter events, 83.9 us)
Async XLA Ops:
  3.5 6.3 %collective-permute-start.4 = (f32[10,68]{1,0:T(8,128)S(1)}, f32[10,68]{1,0:T(8,128)S(1)}, u32[]{:S(2)}, u32[]{:S(2)}) collective-permute-start(f32[10,68]{1,0:T(8,128)S(1)} %bitcast.89), channel_id=1, source_target_pairs={{0,4},{4,8},{8,12},{12,16},{16,20},{20,24},{24,28},{28,0},{1,5},{5... | collective-permute-start | bytes 8168 | tf_op jit(solution)/shard_map/ppermute | solution.py:85
  5.6 25.0 %collective-permute-start = (f32[10,1,384]{2,1,0:T(1,128)S(1)}, f32[10,1,384]{2,1,0:T(1,128)S(1)}, u32[]{:S(2)}, u32[]{:S(2)}) collective-permute-start(f32[10,1,384]{2,1,0:T(1,128)S(1)} %get-tuple-element.76), channel_id=1, source_target_pairs={{0,4},{4,8},{8,12},{12,16},{16,20},{20,24},{24,28},{28,0},{1,5},{5... | collective-permute-start | bytes 46088 | tf_op jit(solution)/shard_map/ppermute | solution.py:16
  6.9 23.7 %collective-permute-start.1 = (f32[10,1,384]{2,1,0:T(1,128)S(1)}, f32[10,1,384]{2,1,0:T(1,128)S(1)}, u32[]{:S(2)}, u32[]{:S(2)}) collective-permute-start(f32[10,1,384]{2,1,0:T(1,128)S(1)} %get-tuple-element.77), channel_id=1, source_target_pairs={{4,0},{8,4},{12,8},{16,12},{20,16},{24,20},{28,24},{0,28},{5,1},{9... | collective-permute-start | bytes 46088 | tf_op jit(solution)/shard_map/ppermute | solution.py:19
  30.6 11.6 %collective-permute-start.9 = (f32[10,68]{1,0:T(8,128)S(1)}, f32[10,68]{1,0:T(8,128)S(1)}, u32[]{:S(2)}, u32[]{:S(2)}) collective-permute-start(f32[10,68]{1,0:T(8,128)S(1)} %collective-permute-done.8), channel_id=1, source_target_pairs={{0,4},{4,8},{8,12},{12,16},{16,20},{20,24},{24,28},{28,0},{1,5},{5... | collective-permute-start | bytes 8168 | tf_op jit(solution)/shard_map/ppermute | solution.py:85
  30.9 11.3 %collective-permute-start.3 = (f32[10,70,1]{1,2,0:T(1,128)S(1)}, f32[10,70,1]{1,2,0:T(1,128)S(1)}, u32[]{:S(2)}, u32[]{:S(2)}) collective-permute-start(f32[10,70,1]{1,2,0:T(1,128)S(1)} %copy.214), channel_id=1, source_target_pairs={{1,0},{2,1},{3,2},{5,4},{6,5},{7,6},{9,8},{10,9},{11,10},{13,12},{... | collective-permute-start | bytes 8408 | tf_op jit(solution)/shard_map/ppermute | solution.py:19
  39.0 7.5 %collective-permute-start.2 = (f32[10,70,1]{2,1,0:T(8,128)S(1)}, f32[10,70,1]{2,1,0:T(8,128)S(1)}, u32[]{:S(2)}, u32[]{:S(2)}) collective-permute-start(f32[10,70,1]{2,1,0:T(8,128)S(1)} %get-tuple-element.74), channel_id=1, source_target_pairs={{0,1},{1,2},{2,3},{4,5},{5,6},{6,7},{8,9},{9,10},{10,11},{12,13},{... | collective-permute-start | bytes 8408 | tf_op jit(solution)/shard_map/ppermute | solution.py:16
  42.1 5.5 %collective-permute-start.10 = (f32[10,68]{1,0:T(8,128)S(1)}, f32[10,68]{1,0:T(8,128)S(1)}, u32[]{:S(2)}, u32[]{:S(2)}) collective-permute-start(f32[10,68]{1,0:T(8,128)S(1)} %collective-permute-done.9), channel_id=1, source_target_pairs={{0,4},{4,8},{8,12},{12,16},{16,20},{20,24},{24,28},{28,0},{1,5},{5... | collective-permute-start | bytes 8168 | tf_op jit(solution)/shard_map/ppermute | solution.py:85
  71.1 10.3 %collective-permute-start.11 = (f32[8,1,384]{2,0,1:T(8,128)S(1)}, f32[8,1,384]{2,0,1:T(8,128)S(1)}, u32[]{:S(2)}, u32[]{:S(2)}) collective-permute-start(f32[8,1,384]{2,0,1:T(8,128)S(1)} %copy.189), channel_id=1, source_target_pairs={{0,4},{4,8},{8,12},{12,16},{16,20},{20,24},{24,28},{28,0},{1,5},{5... | collective-permute-start | bytes 36872 | tf_op jit(solution)/shard_map/ppermute | solution.py:16
  71.2 10.8 %collective-permute-start.12 = (f32[8,1,384]{2,0,1:T(8,128)S(1)}, f32[8,1,384]{2,0,1:T(8,128)S(1)}, u32[]{:S(2)}, u32[]{:S(2)}) collective-permute-start(f32[8,1,384]{2,0,1:T(8,128)S(1)} %copy.190), channel_id=1, source_target_pairs={{4,0},{8,4},{12,8},{16,12},{20,16},{24,20},{28,24},{0,28},{5,1},{9... | collective-permute-start | bytes 36872 | tf_op jit(solution)/shard_map/ppermute | solution.py:19
  81.4 15.7 %collective-permute-start.20 = (f32[8,68]{1,0:T(8,128)S(1)}, f32[8,68]{1,0:T(8,128)S(1)}, u32[]{:S(2)}, u32[]{:S(2)}) collective-permute-start(f32[8,68]{1,0:T(8,128)S(1)} %collective-permute-done.19), channel_id=1, source_target_pairs={{0,4},{4,8},{8,12},{12,16},{16,20},{20,24},{24,28},{28,0},{1,5},{5... | collective-permute-start | bytes 6536 | tf_op jit(solution)/shard_map/ppermute | solution.py:85
  84.6 12.6 %collective-permute-start.13 = (f32[8,70,1]{1,0,2:T(8,128)S(1)}, f32[8,70,1]{1,0,2:T(8,128)S(1)}, u32[]{:S(2)}, u32[]{:S(2)}) collective-permute-start(f32[8,70,1]{1,0,2:T(8,128)S(1)} %get-tuple-element.70), channel_id=1, source_target_pairs={{0,1},{1,2},{2,3},{4,5},{5,6},{6,7},{8,9},{9,10},{10,11},{12,13},{... | collective-permute-start | bytes 6728 | tf_op jit(solution)/shard_map/ppermute | solution.py:16
  97.1 5.5 %collective-permute-start.21 = (f32[8,68]{1,0:T(8,128)S(1)}, f32[8,68]{1,0:T(8,128)S(1)}, u32[]{:S(2)}, u32[]{:S(2)}) collective-permute-start(f32[8,68]{1,0:T(8,128)S(1)} %collective-permute-done.20), channel_id=1, source_target_pairs={{0,4},{4,8},{8,12},{12,16},{16,20},{20,24},{24,28},{28,0},{1,5},{5... | collective-permute-start | bytes 6536 | tf_op jit(solution)/shard_map/ppermute | solution.py:85
  107.5 30.6 %collective-permute-start.22 = (f32[8,1,384]{2,0,1:T(8,128)S(1)}, f32[8,1,384]{2,0,1:T(8,128)S(1)}, u32[]{:S(2)}, u32[]{:S(2)}) collective-permute-start(f32[8,1,384]{2,0,1:T(8,128)S(1)} %copy.197), channel_id=1, source_target_pairs={{0,4},{4,8},{8,12},{12,16},{16,20},{20,24},{24,28},{28,0},{1,5},{5... | collective-permute-start | bytes 36872 | tf_op jit(solution)/shard_map/ppermute | solution.py:16
  107.6 31.1 %collective-permute-start.23 = (f32[8,1,384]{2,0,1:T(8,128)S(1)}, f32[8,1,384]{2,0,1:T(8,128)S(1)}, u32[]{:S(2)}, u32[]{:S(2)}) collective-permute-start(f32[8,1,384]{2,0,1:T(8,128)S(1)} %copy.198), channel_id=1, source_target_pairs={{4,0},{8,4},{12,8},{16,12},{20,16},{24,20},{28,24},{0,28},{5,1},{9... | collective-permute-start | bytes 36872 | tf_op jit(solution)/shard_map/ppermute | solution.py:19
  112.1 5.4 %collective-permute-start.26 = (f32[8,68]{1,0:T(8,128)S(1)}, f32[8,68]{1,0:T(8,128)S(1)}, u32[]{:S(2)}, u32[]{:S(2)}) collective-permute-start(f32[8,68]{1,0:T(8,128)S(1)} %slice_reduce_fusion.1), channel_id=1, source_target_pairs={{0,4},{4,8},{8,12},{12,16},{16,20},{20,24},{24,28},{28,0},{1,5},{5... | collective-permute-start | bytes 6536 | tf_op jit(solution)/shard_map/ppermute | solution.py:85
  138.1 15.7 %collective-permute-start.31 = (f32[8,68]{1,0:T(8,128)S(1)}, f32[8,68]{1,0:T(8,128)S(1)}, u32[]{:S(2)}, u32[]{:S(2)}) collective-permute-start(f32[8,68]{1,0:T(8,128)S(1)} %collective-permute-done.30), channel_id=1, source_target_pairs={{0,4},{4,8},{8,12},{12,16},{16,20},{20,24},{24,28},{28,0},{1,5},{5... | collective-permute-start | bytes 6536 | tf_op jit(solution)/shard_map/ppermute | solution.py:85
  141.3 12.6 %collective-permute-start.24 = (f32[8,70,1]{1,0,2:T(8,128)S(1)}, f32[8,70,1]{1,0,2:T(8,128)S(1)}, u32[]{:S(2)}, u32[]{:S(2)}) collective-permute-start(f32[8,70,1]{1,0,2:T(8,128)S(1)} %get-tuple-element.68), channel_id=1, source_target_pairs={{0,1},{1,2},{2,3},{4,5},{5,6},{6,7},{8,9},{9,10},{10,11},{12,13},{... | collective-permute-start | bytes 6728 | tf_op jit(solution)/shard_map/ppermute | solution.py:16
  153.8 5.5 %collective-permute-start.32 = (f32[8,68]{1,0:T(8,128)S(1)}, f32[8,68]{1,0:T(8,128)S(1)}, u32[]{:S(2)}, u32[]{:S(2)}) collective-permute-start(f32[8,68]{1,0:T(8,128)S(1)} %collective-permute-done.31), channel_id=1, source_target_pairs={{0,4},{4,8},{8,12},{12,16},{16,20},{20,24},{24,28},{28,0},{1,5},{5... | collective-permute-start | bytes 6536 | tf_op jit(solution)/shard_map/ppermute | solution.py:85
  164.3 30.6 %collective-permute-start.33 = (f32[8,1,384]{2,0,1:T(8,128)S(1)}, f32[8,1,384]{2,0,1:T(8,128)S(1)}, u32[]{:S(2)}, u32[]{:S(2)}) collective-permute-start(f32[8,1,384]{2,0,1:T(8,128)S(1)} %copy.205), channel_id=1, source_target_pairs={{0,4},{4,8},{8,12},{12,16},{16,20},{20,24},{24,28},{28,0},{1,5},{5... | collective-permute-start | bytes 36872 | tf_op jit(solution)/shard_map/ppermute | solution.py:16
  164.4 31.1 %collective-permute-start.34 = (f32[8,1,384]{2,0,1:T(8,128)S(1)}, f32[8,1,384]{2,0,1:T(8,128)S(1)}, u32[]{:S(2)}, u32[]{:S(2)}) collective-permute-start(f32[8,1,384]{2,0,1:T(8,128)S(1)} %copy.206), channel_id=1, source_target_pairs={{4,0},{8,4},{12,8},{16,12},{20,16},{24,20},{28,24},{0,28},{5,1},{9... | collective-permute-start | bytes 36872 | tf_op jit(solution)/shard_map/ppermute | solution.py:19
  174.1 5.4 %collective-permute-start.38 = (f32[8,68]{1,0:T(8,128)S(1)}, f32[8,68]{1,0:T(8,128)S(1)}, u32[]{:S(2)}, u32[]{:S(2)}) collective-permute-start(f32[8,68]{1,0:T(8,128)S(1)} %collective-permute-done.37), channel_id=1, source_target_pairs={{0,4},{4,8},{8,12},{12,16},{16,20},{20,24},{24,28},{28,0},{1,5},{5... | collective-permute-start | bytes 6536 | tf_op jit(solution)/shard_map/ppermute | solution.py:85
  194.9 15.7 %collective-permute-start.42 = (f32[8,68]{1,0:T(8,128)S(1)}, f32[8,68]{1,0:T(8,128)S(1)}, u32[]{:S(2)}, u32[]{:S(2)}) collective-permute-start(f32[8,68]{1,0:T(8,128)S(1)} %collective-permute-done.41), channel_id=1, source_target_pairs={{0,4},{4,8},{8,12},{12,16},{16,20},{20,24},{24,28},{28,0},{1,5},{5... | collective-permute-start | bytes 6536 | tf_op jit(solution)/shard_map/ppermute | solution.py:85
  198.1 12.7 %collective-permute-start.35 = (f32[8,70,1]{1,0,2:T(8,128)S(1)}, f32[8,70,1]{1,0,2:T(8,128)S(1)}, u32[]{:S(2)}, u32[]{:S(2)}) collective-permute-start(f32[8,70,1]{1,0,2:T(8,128)S(1)} %get-tuple-element.66), channel_id=1, source_target_pairs={{0,1},{1,2},{2,3},{4,5},{5,6},{6,7},{8,9},{9,10},{10,11},{12,13},{... | collective-permute-start | bytes 6728 | tf_op jit(solution)/shard_map/ppermute | solution.py:16
  210.7 5.5 %collective-permute-start.43 = (f32[8,68]{1,0:T(8,128)S(1)}, f32[8,68]{1,0:T(8,128)S(1)}, u32[]{:S(2)}, u32[]{:S(2)}) collective-permute-start(f32[8,68]{1,0:T(8,128)S(1)} %collective-permute-done.42), channel_id=1, source_target_pairs={{0,4},{4,8},{8,12},{12,16},{16,20},{20,24},{24,28},{28,0},{1,5},{5... | collective-permute-start | bytes 6536 | tf_op jit(solution)/shard_map/ppermute | solution.py:85
  (47 other events, 297.2 us)
